TPU v7x, 512 devices: a whole 4x8x8 slice. The times are simulated.
512 devices in a mesh: mod: 512 (over y, z, x, core).
Axes of the slice: x: 4, y: 8, z: 8, core: 2. Of those that a mesh axis runs over, the one named last changes fastest.
Arguments:
- loads: bfloat16 [32, 524288], P(None, 'mod')
- modes: float32 [6, 524288], P(None, 'mod'), may hold values from -0.6 to 0.6
- pinv: bfloat16 [524288, 1024], P('mod')
- schur: bfloat16 [524288, 1024], P('mod')
- coarse_inverse: float32 [3072, 3072], P('mod')
- connectors: int32 [512, 3, 8], P('mod'), may hold values from -1 to 4, as said below
Outputs:
- multipliers: float32 [32, 524288], P(None, 'mod')
Inputs may be any that keep to these rules, and one draw needn't show every extreme that they name: connectors[s, 0, b] is 0 for an unused block, or 1, 2, 3, 4 when the block is tied to module s + 1, s - 1, s + 8, s - 8; its partner is the block of that module with the opposite direction (1 with 2, 3 with 4) and the same slot connectors[s, 1, b], which is below 2 (0 on unused blocks). connectors[s, 2, b] is +1 or -1 on used blocks, opposite at the two ends of a connector, and 0 on unused ones. Partners stay within rows of 8 modules along the first kind of direction and within the modules along the second. A module uses at most 2 blocks towards one neighbour, and some module uses 2.
All inputs are finite; a program needn't handle non-finite values.
Results may differ from a plain program's by a relative error of at most 0.0015.
Values sent between devices are 32-bit elements; how exact they have to be, the bound alone decides.
A program may use at most 64 MiB of HBM per device.

v0:
```python
import jax
import jax.numpy as jnp
from jax import lax
from jax.sharding import PartitionSpec as P

MODES = 6
MAXC = 2
ACROSS = 8


highest = lax.Precision.HIGHEST


def shifted(block, axis, distance):
    devices = range(lax.axis_size(axis))
    route = [(i - distance, i) for i in devices if i - distance in devices]
    return lax.ppermute(block, axis, route)


def on_device(loads, modes, pinv, schur, coarse_inverse, connectors):
    case_count, dof_count = loads.shape
    block_count = connectors.shape[2]
    block_size = dof_count // block_count
    orient = connectors[0, 2].astype(jnp.float32)
    orient_flat = jnp.repeat(orient, block_size)[None, :]
    headings = connectors[0, 0]
    slot_ids = connectors[0, 1]
    heading_ids = jnp.arange(4, dtype=jnp.int32)[:, None, None] + 1
    slot_range = jnp.arange(MAXC, dtype=jnp.int32)[None, :, None]
    selector = (
        (headings[None, None] == heading_ids) & (slot_ids[None, None] == slot_range)
    ).astype(jnp.float32)
    offsets = [1, -1, ACROSS, -ACROSS]
    module_count = coarse_inverse.shape[1] // MODES
    inverse_view = coarse_inverse.reshape(MODES, module_count, MODES)

    def jump_with(values_in, mover):
        signed = values_in.reshape(case_count, block_count, block_size) * orient[None, :, None]
        summed = signed
        for heading in range(4):
            packed = jnp.einsum("kb,cbe->kce", selector[heading ^ 1], signed, precision=highest)
            received = mover(packed, heading)
            summed = summed + jnp.einsum(
                "kb,kce->cbe", selector[heading], received, precision=highest
            )
        return summed.reshape(case_count, dof_count)

    def move_values(packed, heading):
        return shifted(packed, "mod", -offsets[heading])

    def move_lifted(packed, heading):
        return shifted(packed, "mod", -offsets[heading])

    def apply_jump(values_in):
        return jump_with(values_in, move_values)

    def coarse_rhs(values_in):
        return lax.dot_general(modes, values_in, (((1,), (1,)), ((), ())), precision=highest)

    def lift(amplitude):
        return lax.dot_general(amplitude, modes, (((0,), (0,)), ((), ())), precision=highest)

    def jump_lift(amplitude):
        return jump_with(lift(amplitude), move_lifted)

    def absorb(piece):
        amplitude = jnp.einsum("imj,mjc->ic", inverse_view, piece, precision=highest)
        return (amplitude, jnp.sum(piece[:, MODES:], axis=(0, 1)))

    def coarse_solve(right_side, partial_value):
        amplitude, unused = absorb(lax.all_gather(right_side[None], "mod", axis=0, tiled=True))
        total_rho = None if partial_value is None else lax.psum(partial_value, "mod")
        return (amplitude, total_rho)

    def project(values_in, partial_value):
        amplitude, total_rho = coarse_solve(coarse_rhs(orient_flat * values_in), partial_value)
        return (values_in - jump_lift(amplitude), total_rho)

    load_values = loads.astype(jnp.float32)
    first_amplitude, unused_rho = coarse_solve(coarse_rhs(load_values), None)
    multipliers = jump_lift(first_amplitude)
    start = (load_values - orient_flat * multipliers).astype(jnp.bfloat16)
    residual = apply_jump(jnp.dot(start, pinv, preferred_element_type=jnp.float32))
    projected, unused_total = project(residual, None)
    scaled = (orient_flat * projected).astype(jnp.bfloat16)
    smoothed = jnp.dot(scaled, schur, preferred_element_type=jnp.float32)
    partial_value = jnp.sum(scaled.astype(jnp.float32) * smoothed, axis=1)
    corrected, rho = project(apply_jump(smoothed), partial_value)
    lifted = (orient_flat * corrected).astype(jnp.bfloat16)
    response = jnp.dot(lifted, pinv, preferred_element_type=jnp.float32)
    kappa = lax.psum(jnp.sum(lifted.astype(jnp.float32) * response, axis=1), "mod")
    stride = rho / kappa
    multipliers = multipliers + stride[:, None] * corrected
    return multipliers


def solution(mesh):
    in_specs = (
        P(None, "mod"),
        P(None, "mod"),
        P("mod", None),
        P("mod", None),
        P("mod", None),
        P("mod", None, None),
    )
    out_specs = P(None, "mod")
    return jax.shard_map(
        on_device, mesh=mesh, in_specs=in_specs, out_specs=out_specs, check_vma=False
    )
```

profile of v0, /device:TPU:1, one launch (start us, length us, event | category | flops | bytes accessed | tf_op | source)
XLA Modules:
  0.0 439.6 jit_solution(2911055395956350459)
XLA Ops:
  0.0 0.8 slice_bitcast_fusion.5
  0.9 3.7 reshape.144
  4.6 2.0 copy.8
  6.8 79.2 %all-gather.3 = f32[512,6,32]{2,1,0:T(8,128)S(1)} all-gather(f32[1,6,32]{2,1,0:T(8,128)S(1)} %convolution_bitcast_fusion.22), channel_id=2, replica_groups=mesh['mod'=512] {'mod'}, dimensions={0}, use_global_device_ids=true | all-gather | bytes 393984 | tf_op jit(solution)/shard_map/all_gather | solution.py:71
  86.0 1.0 fusion.27
  87.0 0.4 fusion.68
  87.6 0.2 fusion.52
  87.8 2.1 collective-permute-start
  90.0 3.5 collective-permute-start.1
  93.5 0.2 fusion.62
  93.7 1.3 collective-permute-start.2
  95.2 4.0 collective-permute-start.3
  99.3 0.9 collective-permute-done.3
  100.2 0.3 convolution_bitcast_fusion.16
  100.5 0.3 convolution_bitcast_fusion.17
  100.8 0.3 convolution_bitcast_fusion.18
  101.0 0.3 fusion.17
  101.3 0.4 fusion.42
  102.6 3.6 collective-permute-start.7
  106.4 3.3 collective-permute-start.4
  109.8 2.2 collective-permute-start.5
  112.0 1.3 collective-permute-start.6
  113.3 0.3 convolution_bitcast_fusion.12
  113.6 3.1 collective-permute-done.6
  116.6 0.3 convolution_bitcast_fusion.13
  116.9 0.3 convolution_bitcast_fusion.14
  117.2 0.3 fusion.19
  117.6 86.2 %all-gather.4 = f32[512,6,32]{2,1,0:T(8,128)S(1)} all-gather(f32[1,6,32]{2,1,0:T(8,128)S(1)} %convolution_bitcast_fusion.21), channel_id=3, replica_groups=mesh['mod'=512] {'mod'}, dimensions={0}, use_global_device_ids=true | all-gather | bytes 393984 | tf_op jit(solution)/shard_map/all_gather | solution.py:71
  203.8 1.0 fusion.30
  204.9 0.4 fusion.69
  206.0 1.3 collective-permute-start.11
  207.5 2.1 collective-permute-start.8
  209.6 3.5 collective-permute-start.9
  213.1 1.3 collective-permute-start.10
  214.4 0.3 convolution_bitcast_fusion.8
  214.7 3.1 collective-permute-done.10
  217.8 0.3 convolution_bitcast_fusion.9
  218.0 0.3 convolution_bitcast_fusion.10
  218.3 0.3 fusion.21
  218.6 0.5 fusion.70
  220.1 2.0 collective-permute-start.12
  222.0 3.6 collective-permute-start.13
  225.6 1.3 collective-permute-start.14
  226.9 4.0 collective-permute-start.15
  231.1 0.9 collective-permute-done.15
  231.9 0.3 convolution_bitcast_fusion.4
  232.2 0.3 convolution_bitcast_fusion.5
  232.5 0.3 convolution_bitcast_fusion.6
  232.8 0.3 fusion.23
  233.2 86.6 %all-gather.5 = f32[512,6,32]{2,1,0:T(8,128)S(1)} all-gather(f32[1,6,32]{2,1,0:T(8,128)S(1)} %convolution_bitcast_fusion.20), channel_id=4, replica_groups=mesh['mod'=512] {'mod'}, dimensions={0}, use_global_device_ids=true | all-gather | bytes 393984 | tf_op jit(solution)/shard_map/all_gather | solution.py:71
  319.9 1.0 fusion.33
  320.9 0.4 fusion.71
  322.0 1.3 collective-permute-start.19
  323.5 2.1 collective-permute-start.16
  325.6 3.5 collective-permute-start.17
  329.1 1.3 collective-permute-start.18
  330.4 0.3 convolution_bitcast_fusion
  330.7 3.1 collective-permute-done.18
  333.8 0.3 convolution_bitcast_fusion.1
  334.0 0.3 convolution_bitcast_fusion.2
  334.3 0.3 fusion.25
  334.6 0.5 fusion.26
  335.1 103.7 %all-reduce = (f32[32]{0:T(128)S(1)}, f32[32]{0:T(128)S(1)}) all-reduce(f32[32]{0:T(128)S(1)} %get-tuple-element.8, f32[32]{0:T(128)S(1)} %fusion.26), channel_id=1, replica_groups=mesh['mod'=512] {'mod'}, use_global_device_ids=true, to_apply=%region_1.0 | all-reduce | flops 64 | bytes 512 | tf_op jit(solution)/shard_map/psum | solution.py:72
  438.9 0.7 bitcast_add_fusion
  (71 shorter events, 5.1 us)
Async XLA Ops:
  0.0 101.3 %copy-start = (bf16[1024,1024]{1,0:T(8,128)(2,1)S(1)}, bf16[1024,1024]{1,0:T(8,128)(2,1)}, u32[]{:S(2)}) copy-start(bf16[1024,1024]{1,0:T(8,128)(2,1)} %param.8) | copy-start | bytes 6291460
  0.0 6.6 %copy-start.2 = (f32[6,1024]{1,0:T(8,128)S(1)}, f32[6,1024]{1,0:T(8,128)}, u32[]{:S(2)}) copy-start(f32[6,1024]{1,0:T(8,128)} %param.7) | copy-start | bytes 73732
  0.0 6.7 %copy-start.3 = (bf16[32,1024]{1,0:T(8,128)(2,1)S(1)}, bf16[32,1024]{1,0:T(8,128)(2,1)}, u32[]{:S(2)}) copy-start(bf16[32,1024]{1,0:T(8,128)(2,1)} %param.6) | copy-start | bytes 196612
  87.8 13.3 %collective-permute-start = (f32[2,32,128]{2,0,1:T(2,128)S(1)}, f32[2,32,128]{2,0,1:T(2,128)S(1)}, u32[]{:S(2)}, u32[]{:S(2)}) collective-permute-start(f32[2,32,128]{2,0,1:T(2,128)S(1)} %fusion.52), channel_id=1, source_target_pairs={{1,0},{2,1},{3,2},{4,3},{5,4},{6,5},{7,6},{8,7},{9,8},{10,9},{11,1... | collective-permute-start | bytes 98312 | tf_op jit(solution)/shard_map/ppermute | solution.py:17
  90.0 10.7 %collective-permute-start.1 = (f32[2,32,128]{2,0,1:T(2,128)S(1)}, f32[2,32,128]{2,0,1:T(2,128)S(1)}, u32[]{:S(2)}, u32[]{:S(2)}) collective-permute-start(f32[2,32,128]{2,0,1:T(2,128)S(1)} %fusion.57), channel_id=1, source_target_pairs={{0,1},{1,2},{2,3},{3,4},{4,5},{5,6},{6,7},{7,8},{8,9},{9,10},{10,1... | collective-permute-start | bytes 98312 | tf_op jit(solution)/shard_map/ppermute | solution.py:17
  93.7 6.8 %collective-permute-start.2 = (f32[2,32,128]{2,0,1:T(2,128)S(1)}, f32[2,32,128]{2,0,1:T(2,128)S(1)}, u32[]{:S(2)}, u32[]{:S(2)}) collective-permute-start(f32[2,32,128]{2,0,1:T(2,128)S(1)} %fusion.62), channel_id=1, source_target_pairs={{8,0},{9,1},{10,2},{11,3},{12,4},{13,5},{14,6},{15,7},{16,8},{17,9... | collective-permute-start | bytes 98312 | tf_op jit(solution)/shard_map/ppermute | solution.py:17
  95.2 5.0 %collective-permute-start.3 = (f32[2,32,128]{2,0,1:T(2,128)S(1)}, f32[2,32,128]{2,0,1:T(2,128)S(1)}, u32[]{:S(2)}, u32[]{:S(2)}) collective-permute-start(f32[2,32,128]{2,0,1:T(2,128)S(1)} %fusion.67), channel_id=1, source_target_pairs={{0,8},{1,9},{2,10},{3,11},{4,12},{5,13},{6,14},{7,15},{8,16},{9,17... | collective-permute-start | bytes 98312 | tf_op jit(solution)/shard_map/ppermute | solution.py:17
  102.6 10.7 %collective-permute-start.7 = (f32[2,32,128]{2,0,1:T(2,128)S(1)}, f32[2,32,128]{2,0,1:T(2,128)S(1)}, u32[]{:S(2)}, u32[]{:S(2)}) collective-permute-start(f32[2,32,128]{2,0,1:T(2,128)S(1)} %fusion.66), channel_id=1, source_target_pairs={{0,8},{1,9},{2,10},{3,11},{4,12},{5,13},{6,14},{7,15},{8,16},{9,17... | collective-permute-start | bytes 98312 | tf_op jit(solution)/shard_map/ppermute | solution.py:17
  106.4 10.8 %collective-permute-start.4 = (f32[2,32,128]{2,0,1:T(2,128)S(1)}, f32[2,32,128]{2,0,1:T(2,128)S(1)}, u32[]{:S(2)}, u32[]{:S(2)}) collective-permute-start(f32[2,32,128]{2,0,1:T(2,128)S(1)} %fusion.51), channel_id=1, source_target_pairs={{1,0},{2,1},{3,2},{4,3},{5,4},{6,5},{7,6},{8,7},{9,8},{10,9},{11,1... | collective-permute-start | bytes 98312 | tf_op jit(solution)/shard_map/ppermute | solution.py:17
  109.8 7.2 %collective-permute-start.5 = (f32[2,32,128]{2,0,1:T(2,128)S(1)}, f32[2,32,128]{2,0,1:T(2,128)S(1)}, u32[]{:S(2)}, u32[]{:S(2)}) collective-permute-start(f32[2,32,128]{2,0,1:T(2,128)S(1)} %fusion.56), channel_id=1, source_target_pairs={{0,1},{1,2},{2,3},{3,4},{4,5},{5,6},{6,7},{7,8},{8,9},{9,10},{10,1... | collective-permute-start | bytes 98312 | tf_op jit(solution)/shard_map/ppermute | solution.py:17
  112.0 4.7 %collective-permute-start.6 = (f32[2,32,128]{2,0,1:T(2,128)S(1)}, f32[2,32,128]{2,0,1:T(2,128)S(1)}, u32[]{:S(2)}, u32[]{:S(2)}) collective-permute-start(f32[2,32,128]{2,0,1:T(2,128)S(1)} %fusion.61), channel_id=1, source_target_pairs={{8,0},{9,1},{10,2},{11,3},{12,4},{13,5},{14,6},{15,7},{16,8},{17,9... | collective-permute-start | bytes 98312 | tf_op jit(solution)/shard_map/ppermute | solution.py:17
  204.9 13.7 %copy-start.1 = (bf16[1024,1024]{1,0:T(8,128)(2,1)S(1)}, bf16[1024,1024]{1,0:T(8,128)(2,1)}, u32[]{:S(2)}) copy-start(bf16[1024,1024]{1,0:T(8,128)(2,1)} %param.9) | copy-start | bytes 6291460
  206.0 8.4 %collective-permute-start.11 = (f32[2,32,128]{2,0,1:T(2,128)S(1)}, f32[2,32,128]{2,0,1:T(2,128)S(1)}, u32[]{:S(2)}, u32[]{:S(2)}) collective-permute-start(f32[2,32,128]{2,0,1:T(2,128)S(1)} %fusion.65), channel_id=1, source_target_pairs={{0,8},{1,9},{2,10},{3,11},{4,12},{5,13},{6,14},{7,15},{8,16},{9,17... | collective-permute-start | bytes 98312 | tf_op jit(solution)/shard_map/ppermute | solution.py:17
  207.5 10.8 %collective-permute-start.8 = (f32[2,32,128]{2,0,1:T(2,128)S(1)}, f32[2,32,128]{2,0,1:T(2,128)S(1)}, u32[]{:S(2)}, u32[]{:S(2)}) collective-permute-start(f32[2,32,128]{2,0,1:T(2,128)S(1)} %fusion.50), channel_id=1, source_target_pairs={{1,0},{2,1},{3,2},{4,3},{5,4},{6,5},{7,6},{8,7},{9,8},{10,9},{11,1... | collective-permute-start | bytes 98312 | tf_op jit(solution)/shard_map/ppermute | solution.py:17
  209.6 8.4 %collective-permute-start.9 = (f32[2,32,128]{2,0,1:T(2,128)S(1)}, f32[2,32,128]{2,0,1:T(2,128)S(1)}, u32[]{:S(2)}, u32[]{:S(2)}) collective-permute-start(f32[2,32,128]{2,0,1:T(2,128)S(1)} %fusion.55), channel_id=1, source_target_pairs={{0,1},{1,2},{2,3},{3,4},{4,5},{5,6},{6,7},{7,8},{8,9},{9,10},{10,1... | collective-permute-start | bytes 98312 | tf_op jit(solution)/shard_map/ppermute | solution.py:17
  213.1 4.7 %collective-permute-start.10 = (f32[2,32,128]{2,0,1:T(2,128)S(1)}, f32[2,32,128]{2,0,1:T(2,128)S(1)}, u32[]{:S(2)}, u32[]{:S(2)}) collective-permute-start(f32[2,32,128]{2,0,1:T(2,128)S(1)} %fusion.60), channel_id=1, source_target_pairs={{8,0},{9,1},{10,2},{11,3},{12,4},{13,5},{14,6},{15,7},{16,8},{17,9... | collective-permute-start | bytes 98312 | tf_op jit(solution)/shard_map/ppermute | solution.py:17
  220.1 12.7 %collective-permute-start.12 = (f32[2,32,128]{2,0,1:T(2,128)S(1)}, f32[2,32,128]{2,0,1:T(2,128)S(1)}, u32[]{:S(2)}, u32[]{:S(2)}) collective-permute-start(f32[2,32,128]{2,0,1:T(2,128)S(1)} %fusion.49), channel_id=1, source_target_pairs={{1,0},{2,1},{3,2},{4,3},{5,4},{6,5},{7,6},{8,7},{9,8},{10,9},{11,1... | collective-permute-start | bytes 98312 | tf_op jit(solution)/shard_map/ppermute | solution.py:17
  222.0 10.4 %collective-permute-start.13 = (f32[2,32,128]{2,0,1:T(2,128)S(1)}, f32[2,32,128]{2,0,1:T(2,128)S(1)}, u32[]{:S(2)}, u32[]{:S(2)}) collective-permute-start(f32[2,32,128]{2,0,1:T(2,128)S(1)} %fusion.54), channel_id=1, source_target_pairs={{0,1},{1,2},{2,3},{3,4},{4,5},{5,6},{6,7},{7,8},{8,9},{9,10},{10,1... | collective-permute-start | bytes 98312 | tf_op jit(solution)/shard_map/ppermute | solution.py:17
  225.6 6.6 %collective-permute-start.14 = (f32[2,32,128]{2,0,1:T(2,128)S(1)}, f32[2,32,128]{2,0,1:T(2,128)S(1)}, u32[]{:S(2)}, u32[]{:S(2)}) collective-permute-start(f32[2,32,128]{2,0,1:T(2,128)S(1)} %fusion.59), channel_id=1, source_target_pairs={{8,0},{9,1},{10,2},{11,3},{12,4},{13,5},{14,6},{15,7},{16,8},{17,9... | collective-permute-start | bytes 98312 | tf_op jit(solution)/shard_map/ppermute | solution.py:17
  226.9 5.0 %collective-permute-start.15 = (f32[2,32,128]{2,0,1:T(2,128)S(1)}, f32[2,32,128]{2,0,1:T(2,128)S(1)}, u32[]{:S(2)}, u32[]{:S(2)}) collective-permute-start(f32[2,32,128]{2,0,1:T(2,128)S(1)} %fusion.64), channel_id=1, source_target_pairs={{0,8},{1,9},{2,10},{3,11},{4,12},{5,13},{6,14},{7,15},{8,16},{9,17... | collective-permute-start | bytes 98312 | tf_op jit(solution)/shard_map/ppermute | solution.py:17
  322.0 8.4 %collective-permute-start.19 = (f32[2,32,128]{2,0,1:T(2,128)S(1)}, f32[2,32,128]{2,0,1:T(2,128)S(1)}, u32[]{:S(2)}, u32[]{:S(2)}) collective-permute-start(f32[2,32,128]{2,0,1:T(2,128)S(1)} %fusion.63), channel_id=1, source_target_pairs={{0,8},{1,9},{2,10},{3,11},{4,12},{5,13},{6,14},{7,15},{8,16},{9,17... | collective-permute-start | bytes 98312 | tf_op jit(solution)/shard_map/ppermute | solution.py:17
  323.5 10.8 %collective-permute-start.16 = (f32[2,32,128]{2,0,1:T(2,128)S(1)}, f32[2,32,128]{2,0,1:T(2,128)S(1)}, u32[]{:S(2)}, u32[]{:S(2)}) collective-permute-start(f32[2,32,128]{2,0,1:T(2,128)S(1)} %fusion.48), channel_id=1, source_target_pairs={{1,0},{2,1},{3,2},{4,3},{5,4},{6,5},{7,6},{8,7},{9,8},{10,9},{11,1... | collective-permute-start | bytes 98312 | tf_op jit(solution)/shard_map/ppermute | solution.py:17
  325.6 8.4 %collective-permute-start.17 = (f32[2,32,128]{2,0,1:T(2,128)S(1)}, f32[2,32,128]{2,0,1:T(2,128)S(1)}, u32[]{:S(2)}, u32[]{:S(2)}) collective-permute-start(f32[2,32,128]{2,0,1:T(2,128)S(1)} %fusion.53), channel_id=1, source_target_pairs={{0,1},{1,2},{2,3},{3,4},{4,5},{5,6},{6,7},{7,8},{8,9},{9,10},{10,1... | collective-permute-start | bytes 98312 | tf_op jit(solution)/shard_map/ppermute | solution.py:17
  329.1 4.7 %collective-permute-start.18 = (f32[2,32,128]{2,0,1:T(2,128)S(1)}, f32[2,32,128]{2,0,1:T(2,128)S(1)}, u32[]{:S(2)}, u32[]{:S(2)}) collective-permute-start(f32[2,32,128]{2,0,1:T(2,128)S(1)} %fusion.58), channel_id=1, source_target_pairs={{8,0},{9,1},{10,2},{11,3},{12,4},{13,5},{14,6},{15,7},{16,8},{17,9... | collective-permute-start | bytes 98312 | tf_op jit(solution)/shard_map/ppermute | solution.py:17
where the time goes:
time: 440 us
  blocking collectives  356 us (81%)
  starting transfers between devices  48.5 us (11%)
  matrix products  15.1 us (3%)
  waiting for transfers between devices  11.1 us (3%)
  local copies, waits for them, and re-layouts  6.04 us (1%)
    all_gather x3, blocking collectives, coarse_solve(): lax.all_gather(right_side[None], 'mod', axis=0, tiled=True)  252 us
    psum x1, blocking collectives, coarse_solve(): lax.psum(partial_value, 'mod')  104 us
    ppermute x20, starting transfers between devices, shifted(): return lax.ppermute(block, axis, route)  48.5 us
    ppermute x20, waiting for transfers between devices, shifted(): return lax.ppermute(block, axis, route)  11.1 us
  transfers between devices with their start and end apart: 20, of which 5 were waited for; matrix products, arithmetic and copies ran while one was open for 1% of the time, Pallas kernels for 0%

commit v1 on v0

v1 whole, which is shorter than its diff:
```python
import functools

import jax
import jax.numpy as jnp
from jax import lax
from jax.experimental import pallas as pl
from jax.experimental.pallas import tpu as pltpu
from jax.sharding import PartitionSpec as P

MODES = 6
MAXC = 2
ACROSS = 8
MESH = pl.DeviceIdType.MESH
F32 = jnp.float32
BF16 = jnp.bfloat16


def nt(left, right):
    return lax.dot_general(left, right, (((1,), (1,)), ((), ())), preferred_element_type=F32)


def split(values):
    high = values.astype(BF16)
    rest = values - high.astype(F32)
    middle = rest.astype(BF16)
    low = (rest - middle.astype(F32)).astype(BF16)
    return jnp.concatenate([high, middle, low], axis=0)


def merge(stacked):
    rows = stacked.shape[0] // 3
    return stacked[:rows] + (stacked[rows : 2 * rows] + stacked[2 * rows :])


def kernel(
    loads_h, modes_h, pinv_h, schur_h, cinv_h, conn, out,
    loads_v, modes_v, pinv_v, schur_v, dbuf, lbuf, gbuf, hbuf,
    cbuf, zbuf, pbuf, rbuf, abuf, esend, erecv, msend, mrecv, wsend, wrecv,
    fbuf, fsend, mult, field,
    local_sem, send_sem, recv_sem,
):
    me = lax.axis_index("mod")
    c = lax.rem(me, 8)
    row = lax.div(me, 8)
    z = lax.rem(row, 8)
    y = lax.div(row, 8)
    cs = [row * 8 + lax.rem(c + k, 8) for k in range(1, 8)]
    zs = [y * 64 + lax.rem(z + k, 8) * 8 + c for k in range(1, 8)]
    ys = [lax.rem(y + k, 8) * 64 + z * 8 + c for k in range(1, 8)]
    near = [cs[0], cs[6], lax.rem(me + 8, 512), lax.rem(me + 504, 512)]

    sends = []
    stages = []

    def stage():
        stages.append(None)
        return len(stages) - 1

    def send(src, dst, at, to):
        copy = pltpu.make_async_remote_copy(
            src_ref=src, dst_ref=dst, send_sem=send_sem.at[at], recv_sem=recv_sem.at[at],
            device_id=(to,), device_id_type=MESH,
        )
        copy.start()

    def arrived(ref, at):
        pltpu.make_async_copy(ref, ref, recv_sem.at[at]).wait()
        sends.append((ref, at))

    copies = [
        pltpu.make_async_copy(modes_h, modes_v.at[pl.ds(0, MODES)], local_sem.at[0]),
        pltpu.make_async_copy(loads_h, loads_v, local_sem.at[1]),
        pltpu.make_async_copy(pinv_h, pinv_v, local_sem.at[2]),
        pltpu.make_async_copy(schur_h, schur_v, local_sem.at[3]),
        pltpu.make_async_copy(
            cinv_h.at[:, pl.ds(pl.multiple_of(y * 384, 128), 384)], dbuf.at[y, pl.ds(0, MODES)], local_sem.at[4]
        ),
    ]
    for copy in copies:
        copy.start()
    barrier = pltpu.get_barrier_semaphore()
    for peer in cs + zs + ys + near[2:]:
        pl.semaphore_signal(barrier, inc=1, device_id=(peer,), device_id_type=MESH)

    sub = lax.broadcasted_iota(jnp.int32, (8, 128), 0)
    group = lax.broadcasted_iota(jnp.int32, (8, 128), 1) >> 5
    packing = group == (sub & 3)
    sigma = [conn[0, 2, b].astype(F32) for b in range(8)]
    used = [s * s for s in sigma]
    code = [conn[0, 0, b] * MAXC + conn[0, 1, b] for b in range(8)]
    select = [
        [[jnp.where(code[b] == (h + 1) * MAXC + k, 1.0, 0.0).astype(F32) for b in range(8)] for k in range(MAXC)]
        for h in range(4)
    ]

    def pick(blocks, h, k):
        total = select[h][k][0] * blocks[0]
        for b in range(1, 8):
            total = total + select[h][k][b] * blocks[b]
        return total

    def cols(b):
        return pl.ds(b * 128, 128)

    def gather_start(step, right):
        packed = jnp.where(packing, right, 0.0)
        cbuf[step, c, 0:1, :] = jnp.sum(packed[0:4], axis=0, keepdims=True)
        cbuf[step, c, 1:2, :] = jnp.sum(packed[4:8], axis=0, keepdims=True)

    def gather_row(step):
        at = stage()
        for peer in cs:
            send(cbuf.at[step, c], cbuf.at[step, c], at, peer)
        return at

    def gather_plane(step, at_row):
        arrived(cbuf.at[step, pl.ds(0, 7)], at_row)
        zbuf[step, z] = cbuf[step].reshape(16, 128)
        at = stage()
        for peer in zs:
            send(zbuf.at[step, z], zbuf.at[step, z], at, peer)
        return at

    def partial_solve(step, at_plane):
        arrived(zbuf.at[step, pl.ds(0, 7)], at_plane)
        right = zbuf[step].reshape(128, 128)
        both = jnp.dot(lbuf[...], right, precision=lax.Precision.HIGHEST, preferred_element_type=F32)
        own = jnp.zeros((64, 128), F32)
        wide = lax.broadcasted_iota(jnp.int32, (64, 128), 1) >> 5
        for j in range(4):
            own = own + jnp.where(wide == j, both[64 * j : 64 * j + 64], 0.0)
        pbuf[step] = own.reshape(8, 8, 128)
        at = stage()
        for k, peer in enumerate(ys):
            send(pbuf.at[step, lax.rem(y + k + 1, 8)], rbuf.at[step, y], at, peer)
        rbuf[step, y] = pbuf[step, y]
        return at

    def amplitude(step, at_sum):
        arrived(rbuf.at[step, pl.ds(0, 7)], at_sum)
        total = rbuf[step, 0]
        for k in range(1, 8):
            total = total + rbuf[step, k]
        total = total + pltpu.roll(total, 32, axis=1)
        abuf[step, 0] = total + pltpu.roll(total, 64, axis=1)
        at = stage()
        for h in range(4):
            send(abuf.at[step, 0], abuf.at[step, 1 + (h ^ 1)], at, near[h])
        return at

    def lifted_field(step, at_near):
        arrived(abuf.at[step, pl.ds(0, 4)], at_near)
        values = abuf[step].reshape(40, 128)[:, 0:32]
        return lax.dot_general(
            values, gbuf[...], (((0,), (0,)), ((), ())), precision=lax.Precision.HIGHEST, preferred_element_type=F32
        )

    def contributions(step, which, values):
        four = jnp.concatenate([values] * 4, axis=0)
        parts = merge(nt(hbuf[which], four))
        at = stage()
        for h in range(4):
            esend[step, h] = parts[8 + 8 * h : 16 + 8 * h]
            send(esend.at[step, h], erecv.at[step, h ^ 1], at, near[h])
        return parts[0:8], at

    def right_side(step, own, at):
        arrived(erecv.at[step], at)
        return own + ((erecv[step, 0] + erecv[step, 1]) + (erecv[step, 2] + erecv[step, 3]))

    def swap_blocks(step, values):
        blocks = [values[:, 128 * b : 128 * b + 128] for b in range(8)]
        at = stage()
        for h in range(4):
            for k in range(MAXC):
                wsend[step, h, k] = pick(blocks, h, k)
            send(wsend.at[step, h], wrecv.at[step, h ^ 1], at, near[h])
        for b in range(8):
            field[:, cols(b)] = used[b] * blocks[b]
        return at

    def subtract_partners(step, at):
        arrived(wrecv.at[step], at)
        for b in range(8):
            total = field[:, cols(b)]
            for h in range(4):
                for k in range(MAXC):
                    total = total - select[h][k][b] * wrecv[step, h, k]
            field[:, cols(b)] = total

    def operator(which, matrix):
        hbuf[which] = split(merge(nt(split(jnp.concatenate([gbuf[...], jnp.zeros((8, 1024), F32)], axis=0)), matrix[...])))

    def row_sums(values):
        total = values[:, 0:128]
        for b in range(1, 8):
            total = total + values[:, 128 * b : 128 * b + 128]
        return total

    copies[0].wait()
    copies[1].wait()
    small = lax.broadcasted_iota(jnp.int32, (8, 1024), 0) < MODES
    modes = jnp.where(small, modes_v[...], 0.0)
    loads = loads_v[...]
    stacked = split(jnp.concatenate([modes, jnp.zeros((8, 1024), F32)], axis=0))
    gather_start(0, merge(nt(stacked, jnp.concatenate([loads] * 4, axis=0)))[0:8])
    mode_blocks = [modes[:, 128 * b : 128 * b + 128] for b in range(8)]
    for h in range(4):
        for k in range(MAXC):
            msend[h, k] = pick(mode_blocks, h, k)
    pl.semaphore_wait(barrier, 23)
    at = gather_row(0)
    at_modes = stage()
    for h in range(4):
        send(msend.at[h], mrecv.at[h ^ 1], at_modes, near[h])
    at_d = stage()
    for k, peer in enumerate(ys):
        start = pl.multiple_of(lax.rem(y + k + 1, 8) * 384, 128)
        send(cinv_h.at[:, pl.ds(start, 384)], dbuf.at[y, pl.ds(0, MODES)], at_d, peer)
    at = gather_plane(0, at)

    for b in range(8):
        gbuf[0:8, cols(b)] = used[b] * mode_blocks[b]
    arrived(mrecv, at_modes)
    for h in range(4):
        for b in range(8):
            gbuf[8 + 8 * h : 16 + 8 * h, cols(b)] = -(
                select[h][0][b] * mrecv[h, 0] + select[h][1][b] * mrecv[h, 1]
            )

    copies[4].wait()
    arrived(dbuf.at[pl.ds(0, 7), pl.ds(0, MODES)], at_d)
    small = (lax.broadcasted_iota(jnp.int32, (64, 384), 0) & 7) < MODES
    pieces = split(jnp.where(small, dbuf[...].reshape(64, 384), 0.0))
    wide = lax.broadcasted_iota(jnp.int32, (384, 512), 1)
    mode = (wide & 1) * 4 + (wide >> 7)
    source = ((wide & 127) >> 1) * MODES + mode
    order = (source == lax.broadcasted_iota(jnp.int32, (384, 512), 0)) & (mode < MODES)
    moved = merge(jnp.dot(pieces, jnp.where(order, 1.0, 0.0).astype(BF16), preferred_element_type=F32))
    for j in range(4):
        lbuf[64 * j : 64 * j + 64] = moved[:, 128 * j : 128 * j + 128]

    at = partial_solve(0, at)
    copies[2].wait()
    operator(0, pinv_v)
    at = amplitude(0, at)
    field_value = lifted_field(0, at)
    mult[...] = field_value
    start = (loads.astype(F32) - field_value).astype(BF16)

    own, at = contributions(0, 0, start)
    at_w = swap_blocks(0, jnp.dot(start, pinv_v[...], preferred_element_type=F32))
    gather_start(1, right_side(0, own, at))
    at = gather_row(1)
    copies[3].wait()
    operator(1, schur_v)
    at = gather_plane(1, at)
    subtract_partners(0, at_w)
    at = partial_solve(1, at)
    at = amplitude(1, at)
    scaled = (field[...] - lifted_field(1, at)).astype(BF16)

    own, at = contributions(1, 1, scaled)
    smoothed = jnp.dot(scaled, schur_v[...], preferred_element_type=F32)
    at_w = swap_blocks(1, smoothed)
    gather_start(2, right_side(1, own, at))
    at = gather_row(2)
    rho = row_sums(scaled.astype(F32) * smoothed)
    at = gather_plane(2, at)
    subtract_partners(1, at_w)
    at = partial_solve(2, at)
    at = amplitude(2, at)
    corrected = field[...] - lifted_field(2, at)
    field[...] = corrected
    lifted = corrected.astype(BF16)

    response = jnp.dot(lifted, pinv_v[...], preferred_element_type=F32)
    kappa = row_sums(lifted.astype(F32) * response)
    both = jnp.concatenate([rho, kappa, rho, kappa], axis=0)
    total = lax.dot_general(
        jnp.ones((8, 128), F32), both, (((1,), (1,)), ((), ())),
        precision=lax.Precision.HIGHEST, preferred_element_type=F32,
    )
    for turn, (peers, mine) in enumerate(((cs, c), (zs, z), (ys, y))):
        fbuf[turn, mine] = total
        at = stage()
        for peer in peers:
            send(fbuf.at[turn, mine], fbuf.at[turn, mine], at, peer)
        arrived(fbuf.at[turn, pl.ds(0, 7)], at)
        total = fbuf[turn, 0]
        for k in range(1, 8):
            total = total + fbuf[turn, k]
    spread = jnp.concatenate([total] * 4, axis=0)
    lane = lax.broadcasted_iota(jnp.int32, (32, 128), 1)
    case = lax.broadcasted_iota(jnp.int32, (32, 128), 0)
    rho_all = jnp.sum(jnp.where(lane == case, spread, 0.0), axis=1, keepdims=True)
    kappa_all = jnp.sum(jnp.where(lane == case + 32, spread, 0.0), axis=1, keepdims=True)
    stride = rho_all / kappa_all
    for b in range(8):
        out[:, cols(b)] = sigma[b] * (mult[:, cols(b)] + stride * field[:, cols(b)])
    for ref, at in sends:
        pltpu.make_async_copy(ref, ref, send_sem.at[at]).wait()


def on_device(loads, modes, pinv, schur, coarse_inverse, connectors):
    anywhere = pl.BlockSpec(memory_space=pl.ANY)
    vmem = pltpu.VMEM
    n_stages = 23
    return pl.pallas_call(
        kernel,
        out_shape=jax.ShapeDtypeStruct(loads.shape, F32),
        in_specs=[anywhere] * 5 + [pl.BlockSpec(memory_space=pltpu.SMEM)],
        out_specs=pl.BlockSpec(memory_space=pltpu.VMEM),
        scratch_shapes=[
            vmem((32, 1024), BF16),
            vmem((8, 1024), F32),
            vmem((1024, 1024), BF16),
            vmem((1024, 1024), BF16),
            vmem((8, 8, 384), F32),
            vmem((256, 128), F32),
            vmem((40, 1024), F32),
            vmem((2, 144, 1024), BF16),
            vmem((3, 8, 2, 128), F32),
            vmem((3, 8, 16, 128), F32),
            vmem((3, 8, 8, 128), F32),
            vmem((3, 8, 8, 128), F32),
            vmem((3, 5, 8, 128), F32),
            vmem((2, 4, 8, 128), F32),
            vmem((2, 4, 8, 128), F32),
            vmem((4, MAXC, 8, 128), F32),
            vmem((4, MAXC, 8, 128), F32),
            vmem((2, 4, MAXC, 32, 128), F32),
            vmem((2, 4, MAXC, 32, 128), F32),
            vmem((3, 8, 8, 128), F32),
            vmem((8, 128), F32),
            vmem((32, 1024), F32),
            vmem((32, 1024), F32),
            pltpu.SemaphoreType.DMA((5,)),
            pltpu.SemaphoreType.DMA((n_stages,)),
            pltpu.SemaphoreType.DMA((n_stages,)),
        ],
        compiler_params=pltpu.CompilerParams(
            collective_id=0, has_side_effects=True, vmem_limit_bytes=48 * 1024 * 1024
        ),
    )(loads, modes, pinv, schur, coarse_inverse, connectors)


def solution(mesh):
    in_specs = (
        P(None, "mod"),
        P(None, "mod"),
        P("mod", None),
        P("mod", None),
        P("mod", None),
        P("mod", None, None),
    )
    out_specs = P(None, "mod")
    return jax.shard_map(
        on_device, mesh=mesh, in_specs=in_specs, out_specs=out_specs, check_vma=False
    )
```

time: 440 us -> 95.7 us (0.22)
  blocking collectives: 356 us -> 0 us
  Pallas kernels: 0 us -> 88.4 us
  starting transfers between devices: 48.5 us -> 0 us
  matrix products: 15.1 us -> 0 us
  waiting for transfers between devices: 11.1 us -> 0 us
    all_gather x3 -> x0, blocking collectives: 252 us -> none  [coarse_solve(): lax.all_gather(right_side[None], 'mod', axis=0, tiled=True)]
    psum x1 -> x0, blocking collectives: 104 us -> none  [coarse_solve(): lax.psum(partial_value, 'mod')]
    pallas_call x0 -> x1, Pallas kernels: none -> 88.4 us  [on_device(): pl.pallas_call(kernel, out_shape=jax.ShapeDtypeStruct(loads.shape, F32),...]
    ppermute x20 -> x0, starting transfers between devices: 48.5 us -> none  [shifted(): return lax.ppermute(block, axis, route)]
    dot_general x52 -> x0, matrix products: 15.1 us -> none  [the longest x20 5.13 us: jump_with(): jnp.einsum('kb,kce->cbe', selector[heading], received, precision=highest)]
    ppermute x20 -> x0, waiting for transfers between devices: 11.1 us -> none  [shifted(): return lax.ppermute(block, axis, route)]
    unnamed x18 -> x12, local copies, waits for them, and re-layouts: 0.28 us -> 7.01 us
    reshape x2 -> x0, local copies, waits for them, and re-layouts: 5.69 us -> none  [on_device(): inverse_view = coarse_inverse.reshape(MODES, module_count, MODES)]
  transfers between devices with their start and end apart: 20 -> 0, of which waited for: 5 -> 0; matrix products, arithmetic and copies ran while one was open for 1% -> 0% of each run, Pallas kernels for 0% -> 0%
where the time goes in v1:
time: 95.7 us; the launch traced here: 95.4 us
  Pallas kernels  88.4 us (92%)
  local copies, waits for them, and re-layouts  7.01 us (7%)
    pallas_call x1, Pallas kernels, on_device(): pl.pallas_call(kernel, out_shape=jax.ShapeDtypeStruct(loads.shape, F32),...  88.4 us
    unnamed x12, local copies, waits for them, and re-layouts  7.01 us

profile of v1, /device:TPU:1, one launch (start us, length us, event | category | flops | bytes accessed | tf_op | source)
XLA Modules:
  0.0 95.4 jit_solution(10061086885139144348)
XLA Ops:
  0.0 0.7 copy.7.conn
  0.7 0.0 copy-start
  0.7 1.6 %copy-done = bf16[1024,1024]{1,0:T(8,128)(2,1)S(1)} copy-done((bf16[1024,1024]{1,0:T(8,128)(2,1)S(1)}, bf16[1024,1024]{1,0:T(8,128)(2,1)}, u32[]{:S(2)}) %copy-start) | copy-done | bytes 2097176
  2.3 0.0 copy-start.1
  2.3 1.6 %copy-done.1 = bf16[1024,1024]{1,0:T(8,128)(2,1)S(1)} copy-done((bf16[1024,1024]{1,0:T(8,128)(2,1)S(1)}, bf16[1024,1024]{1,0:T(8,128)(2,1)}, u32[]{:S(2)}) %copy-start.1) | copy-done | bytes 2097176
  3.9 0.0 copy-start.2
  3.9 0.9 copy-done.2
  4.8 0.0 copy-start.3
  4.8 0.8 copy-done.3
  5.6 0.0 copy-start.4
  5.6 0.8 copy-done.4
  6.4 88.4 %shard_map.64 = f32[32,1024]{1,0:T(8,128)S(1)} custom-call(bf16[32,1024]{1,0:T(8,128)(2,1)S(1)} %copy-done.3, f32[6,1024]{1,0:T(8,128)S(1)} %copy-done.4, bf16[1024,1024]{1,0:T(8,128)(2,1)S(1)} %copy-done, bf16[1024,1024]{1,0:T(8,128)(2,1)S(1)} %copy-done.1, f32[6,3072]{1,0:T(8,128)S(1)} %copy-done.2, s32[1,3,8]{2,1,0:T(4,128)S(1)} %copy.7.conn), custom_call_target="tpu_custom_call" | custom-call | tf_op jit(solution)/shard_map/pallas_call | solution.py:309
  94.8 0.7 copy.9
Async XLA Ops:
  0.7 1.6 %copy-start = (bf16[1024,1024]{1,0:T(8,128)(2,1)S(1)}, bf16[1024,1024]{1,0:T(8,128)(2,1)}, u32[]{:S(2)}) copy-start(bf16[1024,1024]{1,0:T(8,128)(2,1)} %pinv_h.1) | copy-start | bytes 6291460
  2.3 1.6 %copy-start.1 = (bf16[1024,1024]{1,0:T(8,128)(2,1)S(1)}, bf16[1024,1024]{1,0:T(8,128)(2,1)}, u32[]{:S(2)}) copy-start(bf16[1024,1024]{1,0:T(8,128)(2,1)} %schur_h.1) | copy-start | bytes 6291460
  3.9 0.9 copy-start.2
  4.8 0.8 copy-start.3
  5.6 0.8 copy-start.4
